TPU v7x, 32 devices: a whole 2x2x4 slice. The times are simulated.
32 devices in a mesh: rows: 8 (over z, y), cols: 4 (over x, core).
Axes of the slice: x: 2, y: 2, z: 4, core: 2. Of those that a mesh axis runs over, the one named last changes fastest.
Arguments:
- factor: bfloat16 [4096, 256], P(('rows', 'cols')), may hold values from -0.09375 to 0.09375
- cores: bfloat16 [4, 256, 256], replicated, as said below
- tile_values: bfloat16 [4, 96, 512, 128], P(None, 'rows', 'cols'), may hold values from -56 to 56
- tile_rows: int32 [4, 8, 48], P(None, 'rows', 'cols'), may hold values from 0 to 3
- tile_cols: int32 [4, 8, 48], P(None, 'rows', 'cols'), may hold values from 0 to 7
- tile_counts: int32 [4, 8, 4], P(None, 'rows', 'cols'), may hold values from 3 to 12, as said below
Outputs:
- factor_new: bfloat16 [4096, 256], P(('rows', 'cols'))
- cores_new: float32 [4, 256, 256], replicated
Inputs may be any that keep to these rules, and one draw needn't show every extreme that they name: cores are dominated by their positive diagonals. `tile_counts`: every relation has some device whose 12 slots are all used. `tile_rows`: several slots may name the same tile.
All inputs are finite; a program needn't handle non-finite values.
Results may differ from a plain program's by a relative error of at most 0.0034.
The roundings to bfloat16 on the way count: a program that leaves them out, or rounds other values in their place, can miss the bound.
Values may be sent and summed in bfloat16 or wider, within the bound.
No kernel may reach another device: no remote copies, remote signals or barrier semaphores. Data moves between devices by JAX's collectives and lax.ppermute only.
A program may use at most 128 MiB of HBM per device.

v0:
```python
import jax
import jax.numpy as jnp
from jax import lax
from jax.sharding import PartitionSpec as P

ridge_weight = 0.1


def normal_system(summed_gram_matrix, cores_float32):
    direct_part = jnp.einsum(
        "krs,st,kqt->rq",
        cores_float32,
        summed_gram_matrix,
        cores_float32,
        precision=lax.Precision.HIGHEST,
    )
    reflected_part = jnp.einsum(
        "euh,uc,eca->ha",
        cores_float32,
        summed_gram_matrix,
        cores_float32,
        precision=lax.Precision.HIGHEST,
    )
    return (
        direct_part
        + reflected_part
        + ridge_weight * jnp.eye(summed_gram_matrix.shape[0], dtype=jnp.float32)
    )


def solve_rows(cholesky_lhs, numerator):
    halfway = lax.linalg.triangular_solve(cholesky_lhs, numerator.T, left_side=True, lower=True)
    return lax.linalg.triangular_solve(
        cholesky_lhs, halfway, left_side=True, lower=True, transpose_a=True
    ).T


def whiten(cholesky_new, core_num):
    relations, rank_size, _ = core_num.shape
    stacked = core_num.transpose(1, 0, 2).reshape(rank_size, relations * rank_size)
    halfway = lax.linalg.triangular_solve(cholesky_new, stacked, left_side=True, lower=True)
    flipped = (
        halfway.reshape(rank_size, relations, rank_size)
        .transpose(2, 1, 0)
        .reshape(rank_size, relations * rank_size)
    )
    second = lax.linalg.triangular_solve(cholesky_new, flipped, left_side=True, lower=True)
    return second.reshape(rank_size, relations, rank_size).transpose(1, 2, 0)


def local(factor, cores, tile_values, tile_rows, tile_cols, tile_counts):
    relations, slot_count, tile_size, _ = tile_values.shape
    own_rows, rank_size = factor.shape
    row_ids = tile_rows[:, 0, :]
    col_ids = tile_cols[:, 0, :]
    live_mask = (jnp.arange(slot_count, dtype=jnp.int32)[None, :] < tile_counts[:, 0, :]).astype(
        jnp.float32
    )
    cores_float32 = cores.astype(jnp.float32)
    gram_old = lax.psum(
        jnp.dot(factor.T, factor, preferred_element_type=jnp.float32), ("rows", "cols")
    )
    cholesky_lhs = jnp.linalg.cholesky(normal_system(gram_old, cores_float32))
    col_tiles = lax.all_gather(factor, "rows", axis=0, tiled=True).reshape(-1, tile_size, rank_size)
    col_count = col_tiles.shape[0]
    panel_tiles = lax.axis_size("cols") * own_rows // tile_size
    row_partial = jnp.zeros((panel_tiles, tile_size, relations, rank_size), jnp.float32)
    for relation in range(relations):
        products = jnp.einsum(
            "sij,sjr->sir",
            tile_values[relation],
            col_tiles[col_ids[relation]],
            preferred_element_type=jnp.float32,
        )
        products = products * live_mask[relation][:, None, None]
        row_partial = row_partial.at[row_ids[relation], :, relation].add(products)
    row_partial = row_partial.reshape(panel_tiles * tile_size, relations, rank_size)
    flat_partial = row_partial.reshape(panel_tiles * tile_size, relations * rank_size)
    row_sum = lax.psum_scatter(flat_partial, "cols", scatter_dimension=0, tiled=True)
    direct = row_sum.reshape(own_rows, relations, rank_size)
    numerator = jnp.einsum("eks,kqs->eq", direct, cores_float32, precision=lax.Precision.HIGHEST)
    panel = lax.all_gather(factor, "cols", axis=0, tiled=True)
    rotated = jnp.einsum("pr,krs->pks", panel, cores, preferred_element_type=jnp.float32).astype(
        jnp.bfloat16
    )
    rotated_tiles = rotated.reshape(panel_tiles, tile_size, relations, rank_size)
    col_partial = jnp.zeros((col_count, tile_size, rank_size), jnp.float32)
    for relation in range(relations):
        rotated_selection = rotated_tiles[row_ids[relation], :, relation]
        back_products = jnp.einsum(
            "sij,sir->sjr",
            tile_values[relation],
            rotated_selection,
            preferred_element_type=jnp.float32,
        )
        back_products = back_products * live_mask[relation][:, None, None]
        col_partial = col_partial.at[col_ids[relation]].add(back_products)
    col_partial = col_partial.reshape(col_count * tile_size, rank_size)
    numerator = numerator + lax.psum_scatter(col_partial, "rows", scatter_dimension=0, tiled=True)
    factor_new = solve_rows(cholesky_lhs, numerator).astype(jnp.bfloat16)
    gram_part = jnp.dot(factor_new.T, factor_new, preferred_element_type=jnp.float32)
    col_new = lax.all_gather(factor_new, "rows", axis=0, tiled=True).reshape(
        -1, tile_size, rank_size
    )
    panel_new = lax.all_gather(factor_new, "cols", axis=0, tiled=True).reshape(
        -1, tile_size, rank_size
    )
    core_matrices = []
    for relation in range(relations):
        upper = jnp.einsum(
            "sij,sir->sjr",
            tile_values[relation],
            panel_new[row_ids[relation]],
            preferred_element_type=jnp.float32,
        ).astype(jnp.bfloat16)
        upper = jnp.where(live_mask[relation][:, None, None] > 0, upper, jnp.zeros_like(upper))
        core_matrices.append(
            jnp.einsum(
                "sjr,sjq->rq", upper, col_new[col_ids[relation]], preferred_element_type=jnp.float32
            )
        )
    core_part = jnp.stack(core_matrices, axis=0)
    gram_new = lax.psum(gram_part, ("rows", "cols"))
    core_num = lax.psum(core_part, ("rows", "cols"))
    cores_new = whiten(jnp.linalg.cholesky(gram_new), core_num)
    return (factor_new, cores_new)


def solution(mesh):
    in_specs = (
        P(("rows", "cols"), None),
        P(),
        P(None, "rows", "cols", None),
        P(None, "rows", "cols"),
        P(None, "rows", "cols"),
        P(None, "rows", "cols"),
    )
    out_specs = (P(("rows", "cols"), None), P())
    return jax.shard_map(local, mesh=mesh, in_specs=in_specs, out_specs=out_specs, check_vma=False)
```

profile of v0, /device:TPU:0, one launch (start us, length us, event | category | flops | bytes accessed | tf_op | source)
XLA Modules:
  0.0 483.6 jit_solution(10696427226409059928)
XLA Ops:
  8.1 1.9 fusion.113
  10.0 33.4 %all_gather.12 = bf16[1024,256]{1,0:T(8,128)(2,1)S(1)} all-gather(bf16[128,256]{1,0:T(8,128)(2,1)} %param.9), channel_id=1, replica_groups=mesh['rows'=8,'cols'=4] {'rows'}, dimensions={0}, use_global_device_ids=true | all-gather | bytes 589824 | tf_op jit(solution)/shard_map/all_gather | solution.py:64
  50.8 1.8 multiply_bitcast_fusion.7
  52.7 1.6 multiply_bitcast_fusion.6
  54.3 1.6 multiply_bitcast_fusion.5
  55.9 1.6 multiply_bitcast_fusion.4
  57.4 1.6 copy.35
  59.0 3.1 copy.37
  62.2 1.6 copy.39
  63.8 3.0 copy.41
  67.1 3.2 scatter_fusion
  70.2 3.2 scatter_fusion.1
  73.4 3.2 scatter_fusion.2
  76.6 3.2 scatter_fusion.3
  81.1 1.8 copy.97
  83.8 6.0 %all_gather.13 = bf16[512,256]{1,0:T(8,128)(2,1)S(1)} all-gather(bf16[128,256]{1,0:T(8,128)(2,1)S(1)} %copy-done.9), channel_id=1, replica_groups=mesh['rows'=8,'cols'=4] {'cols'}, dimensions={0}, use_global_device_ids=true | all-gather | bytes 327680 | tf_op jit(solution)/shard_map/all_gather | solution.py:82
  90.9 2.7 multiply_bitcast_fusion.3
  93.6 1.9 copy.47
  97.0 2.8 multiply_bitcast_fusion.2
  99.8 3.1 copy.50
  104.5 2.9 multiply_bitcast_fusion.1
  107.4 3.1 copy.53
  111.9 2.8 multiply_bitcast_fusion
  114.7 3.1 copy.56
  117.9 1.8 scatter_fusion.4
  119.8 3.1 scatter_fusion.5
  122.9 1.8 scatter_fusion.6
  124.8 3.1 scatter_fusion.7
  129.5 22.2 %all-reduce.9.cloned.1.call-done = f32[256,256]{1,0:T(8,128)} async-done(((f32[256,256]{1,0:T(8,128)}), f32[256,256]{1,0:T(8,128)}) %all-reduce.9.cloned.1.call-update) | async-done | bytes 262160 | tf_op jit(solution)/shard_map/psum | solution.py:60
  151.7 1.7 fusion.67
  155.7 11.7 %cholesky.130 = f32[128,128]{1,0:T(8,128)S(1)} custom-call(f32[128,128]{1,0:T(8,128)S(1)} %cholesky.194), custom_call_target="Cholesky" | custom-call | tf_op jit(solution)/shard_map/jit(cholesky)/cholesky | solution.py:63
  167.6 9.8 %custom-call.35 = f32[1,128,128]{1,2,0:T(8,128)S(1)} custom-call(f32[1,128,128]{2,1,0:T(8,128)S(1)} %get-tuple-element.75), custom_call_target="InvertDiagBlocksLowerTriangular" | custom-call | tf_op jit(solution)/shard_map/jit(cholesky)/cholesky | solution.py:63
  178.0 11.9 %cholesky.147 = f32[128,128]{1,0:T(8,128)S(1)} custom-call(f32[128,128]{1,0:T(8,128)S(1)} %convolution_subtract_fusion.5), custom_call_target="Cholesky" | custom-call | tf_op jit(solution)/shard_map/jit(cholesky)/cholesky | solution.py:63
  192.2 4.4 while.5
  196.6 19.7 %custom-call.16 = f32[2,128,128]{1,2,0:T(8,128)S(1)} custom-call(f32[2,128,128]{2,1,0:T(8,128)S(1)} %get-tuple-element.19), custom_call_target="InvertDiagBlocksLowerTriangular" | custom-call | tf_op jit(solution)/shard_map/triangular_solve | solution.py:33
  221.5 27.7 %all_gather.15 = bf16[1024,256]{0,1:T(8,128)(2,1)S(1)} all-gather(bf16[128,256]{0,1:T(8,128)(2,1)S(1)} %fusion.88), channel_id=1, replica_groups=mesh['rows'=8,'cols'=4] {'rows'}, dimensions={0}, use_global_device_ids=true | all-gather | bytes 589824 | tf_op jit(solution)/shard_map/all_gather | solution.py:102
  249.2 5.8 %all_gather.14 = bf16[512,256]{0,1:T(8,128)(2,1)S(1)} all-gather(bf16[128,256]{0,1:T(8,128)(2,1)S(1)} %fusion.88), channel_id=1, replica_groups=mesh['rows'=8,'cols'=4] {'cols'}, dimensions={0}, use_global_device_ids=true | all-gather | bytes 327680 | tf_op jit(solution)/shard_map/all_gather | solution.py:105
  266.5 2.1 fusion.12
  268.5 2.1 fusion.13
  270.6 2.8 fusion.14
  273.4 2.5 fusion.15
  275.9 2.1 pad_maximum_fusion
  278.7 128.2 %all-reduce.11.cloned.1.call-done = (f32[256,1024]{0,1:T(8,128)}, f32[256,256]{0,1:T(8,128)}) async-done(((f32[256,1024]{0,1:T(8,128)}, f32[256,256]{0,1:T(8,128)}), (f32[256,1024]{0,1:T(8,128)}, f32[256,256]{0,1:T(8,128)})) %all-reduce.11.cloned.1.call-update) | async-done | bytes 1310736 | tf_op jit(solution)/shard_map/psum | solution.py:124
  409.0 11.7 %cholesky.164 = f32[128,128]{1,0:T(8,128)S(1)} custom-call(f32[128,128]{1,0:T(8,128)S(1)} %cholesky.197), custom_call_target="Cholesky" | custom-call | tf_op jit(solution)/shard_map/jit(cholesky)/cholesky | solution.py:125
  420.8 9.8 %custom-call.36 = f32[1,128,128]{1,2,0:T(8,128)S(1)} custom-call(f32[1,128,128]{2,1,0:T(8,128)S(1)} %get-tuple-element.73), custom_call_target="InvertDiagBlocksLowerTriangular" | custom-call | tf_op jit(solution)/shard_map/jit(cholesky)/cholesky | solution.py:125
  431.1 11.9 %cholesky.181 = f32[128,128]{1,0:T(8,128)S(1)} custom-call(f32[128,128]{1,0:T(8,128)S(1)} %convolution_subtract_fusion.2), custom_call_target="Cholesky" | custom-call | tf_op jit(solution)/shard_map/jit(cholesky)/cholesky | solution.py:125
  445.7 4.1 while.6
  449.8 19.7 %custom-call.38 = f32[2,128,128]{1,2,0:T(8,128)S(1)} custom-call(f32[2,128,128]{2,1,0:T(8,128)S(1)} %get-tuple-element.27), custom_call_target="InvertDiagBlocksLowerTriangular" | custom-call | tf_op jit(solution)/shard_map/triangular_solve/custom-call.5 | solution.py:47
  (140 shorter events, 57.1 us)
Async XLA Ops:
  8.0 81.8 %copy-start = (bf16[4,256,256]{2,1,0:T(8,128)(2,1)S(1)}, bf16[4,256,256]{2,1,0:T(8,128)(2,1)}, u32[]{:S(2)}) copy-start(bf16[4,256,256]{2,1,0:T(8,128)(2,1)} %param.10) | copy-start | bytes 1572868
  8.0 143.7 %all-reduce.9.cloned.1.call-start = ((), (), s32[]{:S(2)}) async-start(), calls=%async_computation.2 | async-start | bytes 524288 | tf_op jit(solution)/shard_map/psum | solution.py:60
  9.9 206.4 %reduce-scatter.3.cloned.1.call-start = ((), (), s32[]{:S(2)}) async-start(), calls=%async_computation.3 | async-start | bytes 2621440 | tf_op jit(solution)/shard_map/reduce_scatter | solution.py:79
  50.7 1.8 copy-start.4
  50.8 2.0 copy-start.6
  52.6 1.7 copy-start.7
  59.0 3.1 copy-start.3
  82.9 0.8 copy-start.9
  82.9 134.6 %reduce-scatter.5.cloned.1.call-start = ((), (), s32[]{:S(2)}) async-start(), calls=%async_computation.4 | async-start | bytes 1179648 | tf_op jit(solution)/shard_map/reduce_scatter | solution.py:99
  119.8 3.1 copy-start.2
  127.9 1.0 copy-start.1
  128.9 278.0 %all-reduce.11.cloned.1.call-start = ((), (), s32[]{:S(2)}) async-start(), calls=%async_computation.5 | async-start | bytes 2621440 | tf_op jit(solution)/shard_map/psum | solution.py:124
  151.7 2.5 copy-start.8
  263.4 3.0 copy-start.5
  409.0 60.6 %copy-start.10 = (f32[256,1024]{0,1:T(8,128)S(1)}, f32[256,1024]{0,1:T(8,128)}, u32[]{:S(2)}) copy-start(f32[256,1024]{0,1:T(8,128)} %get-tuple-element.56) | copy-start | bytes 3145732
Sparse Core Ops, SparseCore 0:
  14.3 137.2 all-reduce.8
  278.1 128.7 all-reduce.10
Sparse Core Ops, SparseCore 1:
  83.0 32.4 reduce-scatter.2
  129.0 64.6 reduce-scatter.4
where the time goes:
time: 492 us; the launch traced here: 484 us
  waiting for transfers between devices  150 us (30%)
  other arithmetic  137 us (28%)
  blocking collectives  72.9 us (15%)
  local copies, waits for them, and re-layouts  61.2 us (12%)
  matrix products  42.5 us (9%)
  between operations  19.3 us (4%)
    psum x1, waiting for transfers between devices, local(): core_num = lax.psum(core_part, ('rows', 'cols'))  128 us
    another operation x7, other arithmetic, local(): cores_new = whiten(jnp.linalg.cholesky(gram_new), core_num)  34.8 us
    another operation x6, other arithmetic, local(): cholesky_lhs = jnp.linalg.cholesky(normal_system(gram_old, cores_float32))  34.2 us
    all_gather x1, blocking collectives, local(): lax.all_gather(factor, 'rows', axis=0, tiled=True)  33.4 us
    all_gather x1, blocking collectives, local(): lax.all_gather(factor_new, 'rows', axis=0, tiled=True)  27.7 us
    psum x1, waiting for transfers between devices, local(): lax.psum(jnp.dot(factor.T, factor, preferred_element_type=jnp.float32), (...  22.2 us
    another operation x3, other arithmetic, whiten(): lax.linalg.triangular_solve(cholesky_new, flipped, left_side=True, lower=...  19.8 us
    another operation x3, other arithmetic, solve_rows(): lax.linalg.triangular_solve(cholesky_lhs, halfway, left_side=True, lower=...  19.7 us
  transfers between devices with their start and end apart: 4, of which 2 were waited for; matrix products, arithmetic and copies ran while one was open for 29% of the time, Pallas kernels for 0%

commit v1 on v0

--- a/solution.py
+++ b/solution.py
@@ -4,6 +4,24 @@
 from jax.sharding import PartitionSpec as P
 
 ridge_weight = 0.1
+
+
+def ring_gather(value, axis, dim):
+    ways, here, step = (lax.axis_size(axis), lax.axis_index(axis), value.shape[dim])
+    shape = [n * ways if d == dim else n for d, n in enumerate(value.shape)]
+    full = lax.dynamic_update_slice_in_dim(
+        jnp.zeros(shape, value.dtype), value, here * step, axis=dim
+    )
+    going_up = going_down = value
+    for far in range(1, ways // 2 + 1):
+        going_up = lax.ppermute(going_up, axis, [(d, (d + 1) % ways) for d in range(ways)])
+        full = lax.dynamic_update_slice_in_dim(full, going_up, (here - far) % ways * step, axis=dim)
+        if 2 * far < ways:
+            going_down = lax.ppermute(going_down, axis, [(d, (d - 1) % ways) for d in range(ways)])
+            full = lax.dynamic_update_slice_in_dim(
+                full, going_down, (here + far) % ways * step, axis=dim
+            )
+    return full
 
 
 def normal_system(summed_gram_matrix, cores_float32):
@@ -61,7 +79,7 @@
         jnp.dot(factor.T, factor, preferred_element_type=jnp.float32), ("rows", "cols")
     )
     cholesky_lhs = jnp.linalg.cholesky(normal_system(gram_old, cores_float32))
-    col_tiles = lax.all_gather(factor, "rows", axis=0, tiled=True).reshape(-1, tile_size, rank_size)
+    col_tiles = ring_gather(factor, "rows", 0).reshape(-1, tile_size, rank_size)
     col_count = col_tiles.shape[0]
     panel_tiles = lax.axis_size("cols") * own_rows // tile_size
     row_partial = jnp.zeros((panel_tiles, tile_size, relations, rank_size), jnp.float32)

time: 492 us -> 484 us (0.984)
  blocking collectives: 72.9 us -> 39.6 us
  starting transfers between devices: 0.63 us -> 16.2 us
  waiting for transfers between devices: 150 us -> 159 us
    all_gather x1 -> x0, blocking collectives: 33.4 us -> none  [local(): lax.all_gather(factor, 'rows', axis=0, tiled=True)]
    ppermute x0 -> x7, starting transfers between devices: none -> 15.6 us  [the longest x3 12.5 us: ring_gather(): lax.ppermute(going_down, axis, [(d, (d - 1) % ways) for d in range(ways)])]
    ppermute x0 -> x7, waiting for transfers between devices: none -> 11.5 us  [the longest x4 11.5 us: ring_gather(): lax.ppermute(going_up, axis, [(d, (d + 1) % ways) for d in range(ways)])]
  transfers between devices with their start and end apart: 4 -> 11, of which waited for: 2 -> 5; matrix products, arithmetic and copies ran while one was open for 29% -> 31% of each run, Pallas kernels for 0% -> 0%
where the time goes in v1:
time: 484 us; the launch traced here: 475 us
  waiting for transfers between devices  159 us (33%)
  other arithmetic  137 us (28%)
  local copies, waits for them, and re-layouts  61.8 us (13%)
  matrix products  42.6 us (9%)
  blocking collectives  39.6 us (8%)
  between operations  19.4 us (4%)
  starting transfers between devices  16.2 us (3%)
    psum x1, waiting for transfers between devices, local(): core_num = lax.psum(core_part, ('rows', 'cols'))  128 us
    another operation x7, other arithmetic, local(): cores_new = whiten(jnp.linalg.cholesky(gram_new), core_num)  34.8 us
    another operation x6, other arithmetic, local(): cholesky_lhs = jnp.linalg.cholesky(normal_system(gram_old, cores_float32))  34.1 us
    all_gather x1, blocking collectives, local(): lax.all_gather(factor_new, 'rows', axis=0, tiled=True)  27.6 us
    another operation x3, other arithmetic, whiten(): lax.linalg.triangular_solve(cholesky_new, flipped, left_side=True, lower=...  19.8 us
    another operation x3, other arithmetic, solve_rows(): lax.linalg.triangular_solve(cholesky_lhs, halfway, left_side=True, lower=...  19.7 us
    psum x1, waiting for transfers between devices, local(): lax.psum(jnp.dot(factor.T, factor, preferred_element_type=jnp.float32), (...  18.8 us
    scatter-add x4, other arithmetic, local(): row_partial = row_partial.at[row_ids[relation], :, relation].add(products)  12.7 us
  transfers between devices with their start and end apart: 11, of which 5 were waited for; matrix products, arithmetic and copies ran while one was open for 31% of the time, Pallas kernels for 0%

profile of v1, /device:TPU:0, one launch (start us, length us, event | category | flops | bytes accessed | tf_op | source)
XLA Modules:
  0.0 474.9 jit_solution(16954778751375568869)
XLA Ops:
  8.1 3.0 collective-permute-start
  11.1 3.1 collective-permute-start.1
  14.2 1.8 fusion.113
  19.4 4.7 collective-permute-start.3
  24.1 2.3 collective-permute-done.2
  26.4 4.7 collective-permute-start.5
  31.2 2.3 collective-permute-done.4
  33.5 7.0 %collective-permute-done.6 = bf16[128,256]{1,0:T(8,128)(2,1)S(1)} collective-permute-done((bf16[128,256]{1,0:T(8,128)(2,1)S(1)}, bf16[128,256]{1,0:T(8,128)(2,1)S(1)}, u32[]{:S(2)}, u32[]{:S(2)}) %collective-permute-start.6) | collective-permute-done | bytes 65568 | tf_op jit(solution)/shard_map/ppermute | solution.py:17
  45.6 1.8 multiply_bitcast_fusion.7
  53.9 3.2 copy.37
  58.7 3.0 copy.41
  61.9 3.2 scatter_fusion
  65.1 3.2 scatter_fusion.1
  68.3 3.2 scatter_fusion.2
  71.5 3.2 scatter_fusion.3
  76.0 1.8 copy.97
  78.6 6.0 %all_gather.9 = bf16[512,256]{1,0:T(8,128)(2,1)S(1)} all-gather(bf16[128,256]{1,0:T(8,128)(2,1)S(1)} %copy-done.9), channel_id=1, replica_groups=mesh['rows'=8,'cols'=4] {'cols'}, dimensions={0}, use_global_device_ids=true | all-gather | bytes 327680 | tf_op jit(solution)/shard_map/all_gather | solution.py:100
  85.8 2.6 multiply_bitcast_fusion.3
  88.4 1.9 copy.47
  91.8 3.0 multiply_bitcast_fusion.2
  94.8 3.0 copy.50
  99.4 2.9 multiply_bitcast_fusion.1
  102.2 3.1 copy.53
  106.8 2.8 multiply_bitcast_fusion
  109.6 3.1 copy.56
  112.8 1.8 scatter_fusion.4
  114.6 3.1 scatter_fusion.5
  117.8 1.8 scatter_fusion.6
  119.6 3.1 scatter_fusion.7
  124.3 18.8 %all-reduce.9.cloned.1.call-done = f32[256,256]{1,0:T(8,128)} async-done(((f32[256,256]{1,0:T(8,128)}), f32[256,256]{1,0:T(8,128)}) %all-reduce.9.cloned.1.call-update) | async-done | bytes 262160 | tf_op jit(solution)/shard_map/psum | solution.py:78
  147.1 11.7 %cholesky.130 = f32[128,128]{1,0:T(8,128)S(1)} custom-call(f32[128,128]{1,0:T(8,128)S(1)} %cholesky.194), custom_call_target="Cholesky" | custom-call | tf_op jit(solution)/shard_map/jit(cholesky)/cholesky | solution.py:81
  159.0 9.8 %custom-call.35 = f32[1,128,128]{1,2,0:T(8,128)S(1)} custom-call(f32[1,128,128]{2,1,0:T(8,128)S(1)} %get-tuple-element.75), custom_call_target="InvertDiagBlocksLowerTriangular" | custom-call | tf_op jit(solution)/shard_map/jit(cholesky)/cholesky | solution.py:81
  169.4 11.8 %cholesky.147 = f32[128,128]{1,0:T(8,128)S(1)} custom-call(f32[128,128]{1,0:T(8,128)S(1)} %convolution_subtract_fusion.5), custom_call_target="Cholesky" | custom-call | tf_op jit(solution)/shard_map/jit(cholesky)/cholesky | solution.py:81
  183.5 4.2 while.5
  187.8 19.7 %custom-call.16 = f32[2,128,128]{1,2,0:T(8,128)S(1)} custom-call(f32[2,128,128]{2,1,0:T(8,128)S(1)} %get-tuple-element.19), custom_call_target="InvertDiagBlocksLowerTriangular" | custom-call | tf_op jit(solution)/shard_map/triangular_solve | solution.py:51
  212.7 27.6 %all_gather.11 = bf16[1024,256]{0,1:T(8,128)(2,1)S(1)} all-gather(bf16[128,256]{0,1:T(8,128)(2,1)S(1)} %fusion.88), channel_id=1, replica_groups=mesh['rows'=8,'cols'=4] {'rows'}, dimensions={0}, use_global_device_ids=true | all-gather | bytes 589824 | tf_op jit(solution)/shard_map/all_gather | solution.py:120
  240.3 5.9 %all_gather.10 = bf16[512,256]{0,1:T(8,128)(2,1)S(1)} all-gather(bf16[128,256]{0,1:T(8,128)(2,1)S(1)} %fusion.88), channel_id=1, replica_groups=mesh['rows'=8,'cols'=4] {'cols'}, dimensions={0}, use_global_device_ids=true | all-gather | bytes 327680 | tf_op jit(solution)/shard_map/all_gather | solution.py:123
  257.7 2.1 fusion.12
  259.8 2.1 fusion.13
  261.8 2.8 fusion.14
  264.6 2.5 fusion.15
  267.1 2.1 pad_maximum_fusion
  270.0 128.2 %all-reduce.11.cloned.1.call-done = (f32[256,1024]{0,1:T(8,128)}, f32[256,256]{0,1:T(8,128)}) async-done(((f32[256,1024]{0,1:T(8,128)}, f32[256,256]{0,1:T(8,128)}), (f32[256,1024]{0,1:T(8,128)}, f32[256,256]{0,1:T(8,128)})) %all-reduce.11.cloned.1.call-update) | async-done | bytes 1310736 | tf_op jit(solution)/shard_map/psum | solution.py:142
  400.3 11.7 %cholesky.164 = f32[128,128]{1,0:T(8,128)S(1)} custom-call(f32[128,128]{1,0:T(8,128)S(1)} %cholesky.197), custom_call_target="Cholesky" | custom-call | tf_op jit(solution)/shard_map/jit(cholesky)/cholesky | solution.py:143
  412.0 9.8 %custom-call.36 = f32[1,128,128]{1,2,0:T(8,128)S(1)} custom-call(f32[1,128,128]{2,1,0:T(8,128)S(1)} %get-tuple-element.73), custom_call_target="InvertDiagBlocksLowerTriangular" | custom-call | tf_op jit(solution)/shard_map/jit(cholesky)/cholesky | solution.py:143
  422.3 11.9 %cholesky.181 = f32[128,128]{1,0:T(8,128)S(1)} custom-call(f32[128,128]{1,0:T(8,128)S(1)} %convolution_subtract_fusion.2), custom_call_target="Cholesky" | custom-call | tf_op jit(solution)/shard_map/jit(cholesky)/cholesky | solution.py:143
  437.0 4.1 while.6
  441.1 19.7 %custom-call.38 = f32[2,128,128]{1,2,0:T(8,128)S(1)} custom-call(f32[2,128,128]{2,1,0:T(8,128)S(1)} %get-tuple-element.27), custom_call_target="InvertDiagBlocksLowerTriangular" | custom-call | tf_op jit(solution)/shard_map/triangular_solve/custom-call.5 | solution.py:65
  (162 shorter events, 67.6 us)
Async XLA Ops:
  8.0 76.7 %copy-start = (bf16[4,256,256]{2,1,0:T(8,128)(2,1)S(1)}, bf16[4,256,256]{2,1,0:T(8,128)(2,1)}, u32[]{:S(2)}) copy-start(bf16[4,256,256]{2,1,0:T(8,128)(2,1)} %param.10) | copy-start | bytes 1572868
  8.0 135.1 %all-reduce.9.cloned.1.call-start = ((), (), s32[]{:S(2)}) async-start(), calls=%async_computation.2 | async-start | bytes 524288 | tf_op jit(solution)/shard_map/psum | solution.py:78
  8.1 11.3 %collective-permute-start = (bf16[128,256]{1,0:T(8,128)(2,1)}, bf16[128,256]{1,0:T(8,128)(2,1)S(1)}, u32[]{:S(2)}, u32[]{:S(2)}) collective-permute-start(bf16[128,256]{1,0:T(8,128)(2,1)} %param.9), channel_id=1, source_target_pairs={{0,4},{4,8},{8,12},{12,16},{16,20},{20,24},{24,28},{28,0},{1,5},{5... | collective-permute-start | bytes 196616 | tf_op jit(solution)/shard_map/ppermute | solution.py:17
  11.1 8.3 %collective-permute-start.1 = (bf16[128,256]{1,0:T(8,128)(2,1)}, bf16[128,256]{1,0:T(8,128)(2,1)S(1)}, u32[]{:S(2)}, u32[]{:S(2)}) collective-permute-start(bf16[128,256]{1,0:T(8,128)(2,1)} %param.9), channel_id=1, source_target_pairs={{0,28},{4,0},{8,4},{12,8},{16,12},{20,16},{24,20},{28,24},{1,29},{... | collective-permute-start | bytes 196616 | tf_op jit(solution)/shard_map/ppermute | solution.py:20
  16.0 191.4 %reduce-scatter.3.cloned.1.call-start = ((), (), s32[]{:S(2)}) async-start(), calls=%async_computation.3 | async-start | bytes 2621440 | tf_op jit(solution)/shard_map/reduce_scatter | solution.py:97
  19.3 7.1 %collective-permute-start.2 = (bf16[128,256]{1,0:T(8,128)(2,1)S(1)}, bf16[128,256]{1,0:T(8,128)(2,1)S(1)}, u32[]{:S(2)}, u32[]{:S(2)}) collective-permute-start(bf16[128,256]{1,0:T(8,128)(2,1)S(1)} %collective-permute-done), channel_id=1, source_target_pairs={{0,4},{4,8},{8,12},{12,16},{16,20},{20,24},{24,28},{28,0},{1,5},{5... | collective-permute-start | bytes 196616 | tf_op jit(solution)/shard_map/ppermute | solution.py:17
  19.4 7.0 %collective-permute-start.3 = (bf16[128,256]{1,0:T(8,128)(2,1)S(1)}, bf16[128,256]{1,0:T(8,128)(2,1)S(1)}, u32[]{:S(2)}, u32[]{:S(2)}) collective-permute-start(bf16[128,256]{1,0:T(8,128)(2,1)S(1)} %collective-permute-done.1), channel_id=1, source_target_pairs={{0,28},{4,0},{8,4},{12,8},{16,12},{20,16},{24,20},{28,24},{1,29},{... | collective-permute-start | bytes 196616 | tf_op jit(solution)/shard_map/ppermute | solution.py:20
  26.4 7.0 %collective-permute-start.4 = (bf16[128,256]{1,0:T(8,128)(2,1)S(1)}, bf16[128,256]{1,0:T(8,128)(2,1)S(1)}, u32[]{:S(2)}, u32[]{:S(2)}) collective-permute-start(bf16[128,256]{1,0:T(8,128)(2,1)S(1)} %collective-permute-done.2), channel_id=1, source_target_pairs={{0,4},{4,8},{8,12},{12,16},{16,20},{20,24},{24,28},{28,0},{1,5},{5... | collective-permute-start | bytes 196616 | tf_op jit(solution)/shard_map/ppermute | solution.py:17
  26.4 7.0 %collective-permute-start.5 = (bf16[128,256]{1,0:T(8,128)(2,1)S(1)}, bf16[128,256]{1,0:T(8,128)(2,1)S(1)}, u32[]{:S(2)}, u32[]{:S(2)}) collective-permute-start(bf16[128,256]{1,0:T(8,128)(2,1)S(1)} %collective-permute-done.3), channel_id=1, source_target_pairs={{0,28},{4,0},{8,4},{12,8},{16,12},{20,16},{24,20},{28,24},{1,29},{... | collective-permute-start | bytes 196616 | tf_op jit(solution)/shard_map/ppermute | solution.py:20
  33.4 7.0 %collective-permute-start.6 = (bf16[128,256]{1,0:T(8,128)(2,1)S(1)}, bf16[128,256]{1,0:T(8,128)(2,1)S(1)}, u32[]{:S(2)}, u32[]{:S(2)}) collective-permute-start(bf16[128,256]{1,0:T(8,128)(2,1)S(1)} %collective-permute-done.4), channel_id=1, source_target_pairs={{0,4},{4,8},{8,12},{12,16},{16,20},{20,24},{24,28},{28,0},{1,5},{5... | collective-permute-start | bytes 196616 | tf_op jit(solution)/shard_map/ppermute | solution.py:17
  45.6 1.8 copy-start.4
  45.6 2.0 copy-start.7
  47.5 1.7 copy-start.6
  53.9 3.2 copy-start.3
  77.8 0.8 copy-start.9
  77.8 130.9 %reduce-scatter.5.cloned.1.call-start = ((), (), s32[]{:S(2)}) async-start(), calls=%async_computation.4 | async-start | bytes 1179648 | tf_op jit(solution)/shard_map/reduce_scatter | solution.py:117
  114.6 3.1 copy-start.2
  122.8 1.0 copy-start.1
  123.7 274.4 %all-reduce.11.cloned.1.call-start = ((), (), s32[]{:S(2)}) async-start(), calls=%async_computation.5 | async-start | bytes 2621440 | tf_op jit(solution)/shard_map/psum | solution.py:142
  143.1 2.5 copy-start.8
  254.7 3.0 copy-start.5
  400.2 60.6 %copy-start.10 = (f32[256,1024]{0,1:T(8,128)S(1)}, f32[256,1024]{0,1:T(8,128)}, u32[]{:S(2)}) copy-start(f32[256,1024]{0,1:T(8,128)} %get-tuple-element.56) | copy-start | bytes 3145732
Sparse Core Ops, SparseCore 0:
  16.2 126.8 all-reduce.8
  269.3 128.7 all-reduce.10
Sparse Core Ops, SparseCore 1:
  77.9 28.8 reduce-scatter.2
  123.8 61.2 reduce-scatter.4
